TPU v7x, 32 devices: a whole 2x2x4 slice. The times are simulated.
32 devices in a mesh: tiles: 2 (over y), sky: 4 (over x, core), visit: 4 (over z).
Axes of the slice: x: 2, y: 2, z: 4, core: 2. Of those that a mesh axis runs over, the one named last changes fastest.
Arguments:
- sky_model: float32 [512, 4096], P(('tiles', 'sky'), 'visit'), parts along dimension 0, may hold values from -6 to 6
- frames: bfloat16 [16, 128, 2048], P(('tiles', 'visit'), 'sky'), parts along dimension 0, may hold values from -8 to 8
- psf_rows: float32 [16, 5], P('tiles'), parts along dimension 0, may hold values from 0.1 to 1
- psf_cols: float32 [16, 5], P('tiles'), parts along dimension 0, may hold values from 0.1 to 1
- dither: int32 [16, 2], P('tiles'), parts along dimension 0, may hold values from -2 to 2
- footprint: int32 [16, 2], P('tiles'), parts along dimension 0, may hold values from 0 to 128, as said below
- huber_cut: float32 [16], P('tiles'), parts along dimension 0, may hold values from 0.3 to 1.5
Outputs:
- gradient: float32 [512, 4096], P(('tiles', 'sky'), 'visit'), parts along dimension 0
There are 2 independent parts, one for each index of `tiles`. A program takes and returns all parts, laid end to end along the dimension named above; each array names one. Nothing has to cross between parts.
Inputs may be any that keep to these rules, and one draw needn't show every extreme that they name: `footprint`: each row is a visit's first covered frame row and one past its last, the first below the second; some visit starts at row 0 and some ends at row 128.
All inputs are finite; a program needn't handle non-finite values.
Results may differ from a plain program's by a relative error of at most 0.0003.
Values may be sent and summed in bfloat16 or wider, within the bound.
A program may use at most 128 MiB of HBM per device.

v0:
```python
import jax
import jax.numpy as jnp
from jax import lax
from jax.sharding import PartitionSpec as P

TAPS = 5


eps_flux = 0.1
tv_weight = 0.5
dither_bound = 2


def padded_2(value, sides, width):
    for axis, dim in sides:
        count, length = (lax.axis_size(axis), value.shape[dim])
        up = [(i, (i + 1) % count) for i in range(count - 1)]
        down = [(j, i) for i, j in up]
        last = lax.slice_in_dim(value, length - width, length, axis=dim)
        initial = lax.slice_in_dim(value, 0, width, axis=dim)
        before = lax.ppermute(last, axis, up)
        after = lax.ppermute(initial, axis, down)
        value = jnp.concatenate([before, value, after], axis=dim)
    return value


def blur_down(values, offset, kernel, length, along_dim):
    half_taps = TAPS // 2
    margin = half_taps + dither_bound
    accum = None
    for b in range(TAPS):
        begin = offset + (b - half_taps + margin)
        piece = kernel[b] * lax.dynamic_slice_in_dim(values, begin, length, along_dim)
        accum = piece if accum is None else accum + piece
    if along_dim == 0:
        return accum[::2]
    return accum[:, ::2]


def spread_up(small, offset, kernel, extra, along_dim):
    half_taps = TAPS // 2
    margin = half_taps + dither_bound
    blank = jnp.zeros_like(small)
    if along_dim == 0:
        upsampled = jnp.stack([small, blank], 1).reshape(2 * small.shape[0], small.shape[1])
        padding = ((margin + extra, margin + extra), (0, 0))
    else:
        upsampled = jnp.stack([small, blank], 2).reshape(small.shape[0], 2 * small.shape[1])
        padding = ((0, 0), (margin + extra, margin + extra))
    padded = jnp.pad(upsampled, padding)
    length = upsampled.shape[along_dim] + 2 * extra
    accum = None
    for b in range(TAPS):
        begin = margin + half_taps - b - offset
        piece = kernel[b] * lax.dynamic_slice_in_dim(padded, begin, length, along_dim)
        accum = piece if accum is None else accum + piece
    return accum


def flux_divergence(window):
    grad_x = window[1:, :-1] - window[:-1, :-1]
    grad_y = window[:-1, 1:] - window[:-1, :-1]
    magnitude = jnp.sqrt(grad_x * grad_x + grad_y * grad_y + eps_flux)
    flux_u = grad_x / magnitude
    flux_w = grad_y / magnitude
    return flux_u[:-1, 1:] - flux_u[1:, 1:] + (flux_w[1:, :-1] - flux_w[1:, 1:])


def visit_rows(columns, frame, row_shift, kernel, cutoff, first, last, row_start):
    margin = TAPS // 2 + dither_bound
    predicted = blur_down(columns, row_shift, kernel, 2 * frame.shape[0], 0)
    low_index = row_start + jnp.arange(frame.shape[0], dtype=jnp.int32)
    inside = (low_index >= first) & (low_index < last)
    clipped = jnp.where(
        inside[:, None],
        jnp.clip(predicted - frame.astype(jnp.float32), -cutoff, cutoff),
        jnp.zeros_like(predicted),
    )
    return spread_up(clipped, row_shift, kernel, margin, 0)


def fold_rows(summed):
    margin = TAPS // 2 + dither_bound
    edges = jnp.concatenate([summed[:margin], summed[-margin:]], 0)
    arrived = padded_2(edges, (("sky", 0),), margin)
    middle = summed[margin:-margin]
    middle = middle.at[:margin].add(arrived[:margin])
    middle = middle.at[-margin:].add(arrived[-margin:])
    return middle


def on_device(sky_model, frames, psf_rows, psf_cols, dither, footprint, huber_cut):
    margin = TAPS // 2 + dither_bound
    visits = psf_rows.shape[0]
    per_device = frames.shape[0]
    sky_pos = lax.axis_index("sky")
    visit_pos = lax.axis_index("visit")
    row_start = sky_pos * frames.shape[1]
    height = sky_model.shape[0]
    local_width = sky_model.shape[1]
    with_rows = padded_2(sky_model, (("sky", 0),), margin)
    whole = lax.all_gather(with_rows, "visit", axis=1, tiled=True)
    full_width = whole.shape[1]
    padded = jnp.pad(whole, ((0, 0), (margin, margin)))

    def one_visit(j, accum):
        k = visit_pos * per_device + j
        col_shift = dither[k, 1]
        columns = blur_down(padded, col_shift, psf_cols[k], full_width, 1)
        back_rows = visit_rows(
            columns,
            frames[j],
            dither[k, 0],
            psf_rows[k],
            huber_cut[k],
            footprint[k, 0],
            footprint[k, 1],
            row_start,
        )
        return accum + spread_up(back_rows, col_shift, psf_cols[k], 0, 1)

    partial_sum = lax.fori_loop(
        0, per_device, one_visit, jnp.zeros((height + 2 * margin, full_width), jnp.float32)
    )
    summed = lax.psum_scatter(partial_sum, "visit", scatter_dimension=1, tiled=True)
    window = lax.dynamic_slice(
        padded, (margin - 1, visit_pos * local_width + margin - 1), (height + 2, local_width + 2)
    )
    data_term = fold_rows(summed)
    return data_term / jnp.sqrt(jnp.float32(visits)) + tv_weight * flux_divergence(window)


def solution(mesh):
    in_specs = (
        P(("tiles", "sky"), "visit"),
        P(("tiles", "visit"), "sky", None),
        P("tiles", None),
        P("tiles", None),
        P("tiles", None),
        P("tiles", None),
        P("tiles"),
    )
    out_specs = P(("tiles", "sky"), "visit")
    return jax.shard_map(
        on_device, mesh=mesh, in_specs=in_specs, out_specs=out_specs, check_vma=False
    )
```

profile of v0, /device:TPU:1, one launch (start us, length us, event | category | flops | bytes accessed | tf_op | source)
XLA Modules:
  0.0 257.1 jit_solution(7931462190371256638)
XLA Ops:
  7.3 4.5 %collective-permute-start = (f32[4,1024]{1,0:T(4,128)S(1)}, f32[4,1024]{1,0:T(4,128)S(1)}, u32[]{:S(2)}, u32[]{:S(2)}) collective-permute-start(f32[4,1024]{1,0:T(4,128)S(1)} %get-tuple-element.474), channel_id=1, source_target_pairs={{0,4},{4,8},{8,12},{1,5},{5,9},{9,13},{2,6},{6,10},{10,14},{3,7},{... | collective-permute-start | bytes 49160 | tf_op jit(solution)/shard_map/ppermute | solution.py:21
  11.8 1.9 collective-permute-start.1
  13.8 3.1 %collective-permute-done.1 = f32[4,1024]{1,0:T(4,128)S(1)} collective-permute-done((f32[4,1024]{1,0:T(4,128)S(1)}, f32[4,1024]{1,0:T(4,128)S(1)}, u32[]{:S(2)}, u32[]{:S(2)}) %collective-permute-start.1) | collective-permute-done | bytes 16416 | tf_op jit(solution)/shard_map/ppermute | solution.py:22
  16.9 1.7 pad_maximum_fusion
  18.7 29.8 %all-gather.2.cloned.1.call-done = f32[72,4096]{1,0:T(8,128)} async-done(((f32[72,1024]{1,0:T(8,128)}), f32[72,4096]{1,0:T(8,128)}) %all-gather.2.cloned.1.call-update) | async-done | bytes 1179664 | tf_op jit(solution)/shard_map/all_gather | solution.py:102
  48.4 2.7 %copy.16 = f32[72,4096]{0,1:T(8,128)} copy(f32[72,4096]{1,0:T(8,128)} %all-gather.2.cloned.1.call-done) | data formatting | bytes 2359296
  51.2 1.8 pad.45.clone
  53.1 154.2 %while.19 = (s32[]{:T(128)}, f32[72,4096]{0,1:T(8,128)}, s32[]{:T(128)}, f32[8,5]{1,0:T(8,128)}, f32[8,5]{1,0:T(8,128)}, /*index=5*/s32[]{:T(128)}, s32[8,2]{0,1...) while((s32[]{:T(128)}, f32[72,4096]{0,1:T(8,128)}, ...), condition=%wide.region_1.2_spmd.clone, body=%wide.region_0.1_spmd.clone.sunk | while | flops 8732888 | bytes 32507664 | solution.py:122
  83.0 5.7 %multiply_add_fusion.4 = f32[72,4096]{0,1:T(8,128)} fusion(f32[72,4104]{0,1:T(8,128)S(1)} %get-tuple-element.654, s32[]{:T(128)S(6)} %select_n.318, s32[]{:T(128)S(6)} %select_n.319, s32[]{:T(128)S(6)} %select_n.320, s32[]{:T(128)S(6)} %select_n.321, s32[]{:T(128)S(6)} %select_n.322, f32[]{:T(128)} %bitcast.143, f32[]{:T(128)} %bitcast.144, ...), kind=kLoop, calls=%fused_computation.1.clone.1 | loop fusion | flops 2654208 | bytes 7077928 | tf_op jit(solution)/shard_map/while/body/eval_jaxpr/add | solution.py:34
  88.7 5.0 %slice.317 = f32[72,2048]{0,1:T(8,128)S(1)} slice(f32[72,4096]{0,1:T(8,128)} %multiply_add_fusion.4), slice={[0:72:1], [0:4096:2]} | slice | bytes 1179648 | tf_op jit(solution)/shard_map/while/body/eval_jaxpr/slice | solution.py:37
  93.7 5.5 %multiply_add_fusion.5 = f32[64,2048]{0,1:T(8,128)} fusion(f32[72,2048]{0,1:T(8,128)S(1)} %slice.317, s32[]{:T(128)S(6)} %select_n.323, s32[]{:T(128)S(6)} %select_n.324, s32[]{:T(128)S(6)} %select_n.325, s32[]{:T(128)S(6)} %select_n.326, s32[]{:T(128)S(6)} %select_n.327, f32[]{:T(128)} %bitcast.158, f32[]{:T(128)} %bitcast.159, f32[]{:T(128)} %bitcast.160, ...), kind=kLoop, calls=%fused_computation.7.clone.1 | loop fusion | flops 1179648 | bytes 3145768 | tf_op jit(solution)/shard_map/while/body/eval_jaxpr/add | solution.py:34
  99.2 11.0 %slice.318 = f32[32,2048]{0,1:T(8,128)S(1)} slice(f32[64,2048]{0,1:T(8,128)} %multiply_add_fusion.5), slice={[0:64:2], [0:2048:1]} | slice | bytes 524288 | tf_op jit(solution)/shard_map/while/body/eval_jaxpr/slice | solution.py:36
  110.2 2.9 %fusion.31 = f32[32,1,2048]{0,2,1:T(8,128)} fusion(f32[32,2048]{0,1:T(8,128)S(1)} %slice.318, bf16[1,32,2048]{1,2,0:T(8,128)(2,1)} %copy.20, f32[]{:T(128)S(6)} %neg.13, f32[]{:T(128)} %bitcast.163, pred[32]{0:T(512)(128)(4,1)S(1)} %compare_and_fusion.2), kind=kLoop, calls=%fused_computation.6.clone.1 | loop fusion | flops 327680 | bytes 655400 | tf_op jit(solution)/shard_map/while/body/eval_jaxpr/stack | solution.py:45
  113.1 1.6 copy.21
  115.3 4.3 %fusion.32 = f32[72,2048,1]{1,0,2:T(8,128)} fusion(s32[]{:T(128)S(6)} %select_n.317, f32[64,2048]{1,0:T(8,128)S(1)} %reshape.185, s32[]{:T(128)S(6)} %select_n.328, s32[]{:T(128)S(6)} %select_n.329, s32[]{:T(128)S(6)} %select_n.330, s32[]{:T(128)S(6)} %select_n.331, f32[]{:T(128)} %bitcast.158, f32[]{:T(128)} %bitcast.159, f32[]{:T(128)} %bitcast.160, ...), kind=kLoop, calls=%fused_computation.18.clone.1 | loop fusion | flops 1327104 | bytes 1114152 | tf_op jit(solution)/shard_map/while/body/eval_jaxpr/stack | solution.py:48
  119.6 2.2 copy.22
  123.5 5.3 %select_add_fusion.2 = f32[72,4096]{0,1:T(8,128)S(1)} fusion(f32[72,4096]{0,1:T(8,128)S(1)} %copy-done, s32[]{:T(128)S(6)} %select_n.312, s32[]{:T(128)S(6)} %select_n.313, s32[]{:T(128)S(6)} %select_n.314, s32[]{:T(128)S(6)} %select_n.315, s32[]{:T(128)S(6)} %select_n.316, f32[72,4096]{0,1:T(8,128)S(1)} %bitcast.175, f32[]{:T(128)} %bitcast.143, ...), kind=kLoop, calls=%fused_computation.clone.1 | loop fusion | flops 3244032 | bytes 3538985 | tf_op jit(solution)/shard_map/while/body/eval_jaxpr/add | solution.py:120
  128.8 1.3 copy-done.1
  160.0 5.7 %multiply_add_fusion.4 = f32[72,4096]{0,1:T(8,128)} fusion(f32[72,4104]{0,1:T(8,128)S(1)} %get-tuple-element.654, s32[]{:T(128)S(6)} %select_n.318, s32[]{:T(128)S(6)} %select_n.319, s32[]{:T(128)S(6)} %select_n.320, s32[]{:T(128)S(6)} %select_n.321, s32[]{:T(128)S(6)} %select_n.322, f32[]{:T(128)} %bitcast.143, f32[]{:T(128)} %bitcast.144, ...), kind=kLoop, calls=%fused_computation.1.clone.1 | loop fusion | flops 2654208 | bytes 7077928 | tf_op jit(solution)/shard_map/while/body/eval_jaxpr/add | solution.py:34
  165.7 5.0 %slice.317 = f32[72,2048]{0,1:T(8,128)S(1)} slice(f32[72,4096]{0,1:T(8,128)} %multiply_add_fusion.4), slice={[0:72:1], [0:4096:2]} | slice | bytes 1179648 | tf_op jit(solution)/shard_map/while/body/eval_jaxpr/slice | solution.py:37
  170.8 5.5 %multiply_add_fusion.5 = f32[64,2048]{0,1:T(8,128)} fusion(f32[72,2048]{0,1:T(8,128)S(1)} %slice.317, s32[]{:T(128)S(6)} %select_n.323, s32[]{:T(128)S(6)} %select_n.324, s32[]{:T(128)S(6)} %select_n.325, s32[]{:T(128)S(6)} %select_n.326, s32[]{:T(128)S(6)} %select_n.327, f32[]{:T(128)} %bitcast.158, f32[]{:T(128)} %bitcast.159, f32[]{:T(128)} %bitcast.160, ...), kind=kLoop, calls=%fused_computation.7.clone.1 | loop fusion | flops 1179648 | bytes 3145768 | tf_op jit(solution)/shard_map/while/body/eval_jaxpr/add | solution.py:34
  176.2 11.0 %slice.318 = f32[32,2048]{0,1:T(8,128)S(1)} slice(f32[64,2048]{0,1:T(8,128)} %multiply_add_fusion.5), slice={[0:64:2], [0:2048:1]} | slice | bytes 524288 | tf_op jit(solution)/shard_map/while/body/eval_jaxpr/slice | solution.py:36
  187.3 2.9 %fusion.31 = f32[32,1,2048]{0,2,1:T(8,128)} fusion(f32[32,2048]{0,1:T(8,128)S(1)} %slice.318, bf16[1,32,2048]{1,2,0:T(8,128)(2,1)} %copy.20, f32[]{:T(128)S(6)} %neg.13, f32[]{:T(128)} %bitcast.163, pred[32]{0:T(512)(128)(4,1)S(1)} %compare_and_fusion.2), kind=kLoop, calls=%fused_computation.6.clone.1 | loop fusion | flops 327680 | bytes 655400 | tf_op jit(solution)/shard_map/while/body/eval_jaxpr/stack | solution.py:45
  190.1 1.6 copy.21
  192.4 4.3 %fusion.32 = f32[72,2048,1]{1,0,2:T(8,128)} fusion(s32[]{:T(128)S(6)} %select_n.317, f32[64,2048]{1,0:T(8,128)S(1)} %reshape.185, s32[]{:T(128)S(6)} %select_n.328, s32[]{:T(128)S(6)} %select_n.329, s32[]{:T(128)S(6)} %select_n.330, s32[]{:T(128)S(6)} %select_n.331, f32[]{:T(128)} %bitcast.158, f32[]{:T(128)} %bitcast.159, f32[]{:T(128)} %bitcast.160, ...), kind=kLoop, calls=%fused_computation.18.clone.1 | loop fusion | flops 1327104 | bytes 1114152 | tf_op jit(solution)/shard_map/while/body/eval_jaxpr/stack | solution.py:48
  196.7 2.2 copy.22
  200.5 5.4 %select_add_fusion.2 = f32[72,4096]{0,1:T(8,128)S(1)} fusion(f32[72,4096]{0,1:T(8,128)S(1)} %copy-done, s32[]{:T(128)S(6)} %select_n.312, s32[]{:T(128)S(6)} %select_n.313, s32[]{:T(128)S(6)} %select_n.314, s32[]{:T(128)S(6)} %select_n.315, s32[]{:T(128)S(6)} %select_n.316, f32[72,4096]{0,1:T(8,128)S(1)} %bitcast.175, f32[]{:T(128)} %bitcast.143, ...), kind=kLoop, calls=%fused_computation.clone.1 | loop fusion | flops 3244032 | bytes 3538985 | tf_op jit(solution)/shard_map/while/body/eval_jaxpr/add | solution.py:120
  207.3 2.8 %copy.12 = f32[72,4096]{1,0:T(8,128)} copy(f32[72,4096]{0,1:T(8,128)} %get-tuple-element.382) | data formatting | bytes 2359296 | tf_op jit(solution)/shard_map/while | solution.py:122
  210.2 28.8 %reduce-scatter.2.cloned.1.call-done = f32[72,1024]{1,0:T(8,128)} async-done(((f32[72,4096]{1,0:T(8,128)}), f32[72,1024]{1,0:T(8,128)}) %reduce-scatter.2.cloned.1.call-update) | async-done | bytes 294928 | tf_op jit(solution)/shard_map/reduce_scatter | solution.py:125
  239.8 3.8 %collective-permute-start.2 = (f32[4,1024]{1,0:T(4,128)S(1)}, f32[4,1024]{1,0:T(4,128)S(1)}, u32[]{:S(2)}, u32[]{:S(2)}) collective-permute-start(f32[4,1024]{1,0:T(4,128)S(1)} %get-tuple-element.473), channel_id=1, source_target_pairs={{0,4},{4,8},{8,12},{1,5},{5,9},{9,13},{2,6},{6,10},{10,14},{3,7},{... | collective-permute-start | bytes 49160 | tf_op jit(solution)/shard_map/ppermute | solution.py:21
  244.2 1.9 collective-permute-start.3
  247.9 1.4 collective-permute-done.3
  (53 shorter events, 22.0 us)
Async XLA Ops:
  6.5 41.9 %all-gather.2.cloned.1.call-start = ((), (), s32[]{:S(2)}) async-start(), calls=%async_computation.1 | async-start | bytes 1474560 | tf_op jit(solution)/shard_map/all_gather | solution.py:102
  7.3 6.4 %collective-permute-start = (f32[4,1024]{1,0:T(4,128)S(1)}, f32[4,1024]{1,0:T(4,128)S(1)}, u32[]{:S(2)}, u32[]{:S(2)}) collective-permute-start(f32[4,1024]{1,0:T(4,128)S(1)} %get-tuple-element.474), channel_id=1, source_target_pairs={{0,4},{4,8},{8,12},{1,5},{5,9},{9,13},{2,6},{6,10},{10,14},{3,7},{... | collective-permute-start | bytes 49160 | tf_op jit(solution)/shard_map/ppermute | solution.py:21
  11.8 5.1 %collective-permute-start.1 = (f32[4,1024]{1,0:T(4,128)S(1)}, f32[4,1024]{1,0:T(4,128)S(1)}, u32[]{:S(2)}, u32[]{:S(2)}) collective-permute-start(f32[4,1024]{1,0:T(4,128)S(1)} %get-tuple-element.475), channel_id=1, source_target_pairs={{4,0},{8,4},{12,8},{5,1},{9,5},{13,9},{6,2},{10,6},{14,10},{7,3},{... | collective-permute-start | bytes 49160 | tf_op jit(solution)/shard_map/ppermute | solution.py:22
  18.6 220.4 %reduce-scatter.2.cloned.1.call-start = ((), (), s32[]{:S(2)}) async-start(), calls=%async_computation.2 | async-start | bytes 1474560 | tf_op jit(solution)/shard_map/reduce_scatter | solution.py:125
  51.2 1.9 copy-start.3
  51.2 1.9 copy-start.4
  51.2 1.9 copy-start.5
  51.2 1.9 copy-start.6
  121.9 1.6 copy-start
  128.8 1.3 copy-start.1
  198.9 1.6 copy-start
  206.0 1.3 copy-start.1
  207.3 36.3 %copy-start.2 = (f32[72,4096]{1,0:T(8,128)S(1)}, f32[72,4096]{1,0:T(8,128)}, u32[]{:S(2)}) copy-start(f32[72,4096]{1,0:T(8,128)} %all-gather.2.cloned.1.call-done) | copy-start | bytes 3538948
  239.8 7.4 %collective-permute-start.2 = (f32[4,1024]{1,0:T(4,128)S(1)}, f32[4,1024]{1,0:T(4,128)S(1)}, u32[]{:S(2)}, u32[]{:S(2)}) collective-permute-start(f32[4,1024]{1,0:T(4,128)S(1)} %get-tuple-element.473), channel_id=1, source_target_pairs={{0,4},{4,8},{8,12},{1,5},{5,9},{9,13},{2,6},{6,10},{10,14},{3,7},{... | collective-permute-start | bytes 49160 | tf_op jit(solution)/shard_map/ppermute | solution.py:21
  244.2 5.1 %collective-permute-start.3 = (f32[4,1024]{1,0:T(4,128)S(1)}, f32[4,1024]{1,0:T(4,128)S(1)}, u32[]{:S(2)}, u32[]{:S(2)}) collective-permute-start(f32[4,1024]{1,0:T(4,128)S(1)} %get-tuple-element.472), channel_id=1, source_target_pairs={{4,0},{8,4},{12,8},{5,1},{9,5},{13,9},{6,2},{10,6},{14,10},{7,3},{... | collective-permute-start | bytes 49160 | tf_op jit(solution)/shard_map/ppermute | solution.py:22
Sparse Core Ops, SparseCore 0:
  18.7 29.6 all-gather.1
  210.3 28.6 reduce-scatter.1
where the time goes:
time: 259 us; the launch traced here: 257 us
  local copies, waits for them, and re-layouts  65.4 us (25%)
  waiting for transfers between devices  63.1 us (24%)
  other arithmetic  54.1 us (21%)
  loops' own time  48.8 us (19%)
  between operations  13.5 us (5%)
  starting transfers between devices  12.2 us (5%)
    another operation x1, loops' own time, on_device(): lax.fori_loop(0, per_device, one_visit, jnp.zeros((height + 2 * margin, f...  48.8 us
    all_gather x1, waiting for transfers between devices, on_device(): whole = lax.all_gather(with_rows, 'visit', axis=1, tiled=True)  29.8 us
    reduce_scatter x1, waiting for transfers between devices, on_device(): lax.psum_scatter(partial_sum, 'visit', scatter_dimension=1, tiled=True)  28.8 us
    add x4, other arithmetic, blur_down(): accum = piece if accum is None else accum + piece  22.4 us
    slice x2, local copies, waits for them, and re-layouts, blur_down(): return accum[::2]  22.1 us
    while x12, local copies, waits for them, and re-layouts  11.8 us
    add x2, other arithmetic, one_visit(): return accum + spread_up(back_rows, col_shift, psf_cols[k], 0, 1)  10.7 us
    slice x2, local copies, waits for them, and re-layouts, blur_down(): return accum[:, ::2]  10 us
  transfers between devices with their start and end apart: 6, of which 4 were waited for; matrix products, arithmetic and copies ran while one was open for 1% of the time, Pallas kernels for 0%

commit v1 on v0

v1 whole, which is shorter than its diff:
```python
import functools

import jax
import jax.numpy as jnp
from jax import lax
from jax.experimental import pallas as pl
from jax.experimental.pallas import tpu as pltpu
from jax.sharding import PartitionSpec as P

TAPS = 5
REACH = 4
SHIFTS = 2 * REACH + 1

eps_flux = 0.1
tv_weight = 0.5

ROWS = 8
LANES = 128

NEIGHBOURS = tuple((y, x) for y in (-1, 0, 1) for x in (-1, 0, 1) if (y, x) != (0, 0))


def split_rows(value):
    high = value.astype(jnp.bfloat16)
    low = (value - high.astype(jnp.float32)).astype(jnp.bfloat16)
    return jnp.concatenate([high, low], axis=0)


def selection(shape, source_of):
    row = lax.broadcasted_iota(jnp.int32, shape, 0)
    col = lax.broadcasted_iota(jnp.int32, shape, 1)
    return jnp.where(source_of(row, col), 1.0, 0.0).astype(jnp.bfloat16)


def dot(a, b):
    return jnp.dot(a, b, preferred_element_type=jnp.float32)


def kernel(
    counts,
    model_ref,
    frames_ref,
    rows_ref,
    cols_ref,
    dither_ref,
    footprint_ref,
    cut_ref,
    out_ref,
    grid_ref,
    shifted_ref,
    frame_ref,
    blurred_ref,
    clipped_ref,
    back_ref,
    total_ref,
    whole_ref,
    side_ref,
    end_ref,
    corner_ref,
    local_sem,
    halo_send,
    halo_recv,
    frame_send,
    frame_recv,
    fold_send,
    fold_recv,
):
    sky_count, visit_count = counts
    height, width = out_ref.shape
    per_device, low_rows, low_cols = frame_ref.shape[1:]
    visits = rows_ref.shape[0]
    full_rows, full_cols = grid_ref.shape
    half_rows, half_cols = full_rows // 2, full_cols // 2
    blocks = full_cols // (2 * LANES)
    tile = lax.axis_index("tiles")
    sky = lax.axis_index("sky")
    visit = lax.axis_index("visit")

    def device(y, x):
        return (tile, sky + y, visit + x)

    def exists(y, x):
        ok = None
        for step, at, count in ((y, sky, sky_count), (x, visit, visit_count)):
            if step:
                here = at > 0 if step < 0 else at < count - 1
                ok = here if ok is None else ok & here
        return ok

    def peer_of(o):
        return lax.rem(visit + o, visit_count)

    def row_part(y):
        return (pl.ds(0, ROWS), pl.ds(ROWS, height), pl.ds(ROWS + height, ROWS))[y + 1]

    def col_part(x):
        return (pl.ds(width + LANES, LANES), pl.ds(0, width), pl.ds(width, LANES))[x + 1]

    def edge_of(y, x):
        r = (pl.ds(0, ROWS), pl.ds(0, height), pl.ds(height - ROWS, ROWS))[y + 1]
        c = (pl.ds(0, LANES), pl.ds(0, width), pl.ds(width - LANES, LANES))[x + 1]
        return r, c

    barrier = pltpu.get_barrier_semaphore()

    def greet(o, carry):
        pl.semaphore_signal(
            barrier, inc=1, device_id=(tile, sky, peer_of(o)), device_id_type=pl.DeviceIdType.MESH
        )
        return carry

    lax.fori_loop(1, visit_count, greet, 0)
    for y, x in NEIGHBOURS:
        if y:

            @pl.when(exists(y, x))
            def _():
                pl.semaphore_signal(
                    barrier, inc=1, device_id=device(y, x), device_id_type=pl.DeviceIdType.MESH
                )

    own_model = pltpu.make_async_copy(
        model_ref, grid_ref.at[pl.ds(ROWS, height), pl.ds(0, width)], local_sem.at[0]
    )
    own_model.start()

    def own_frames():
        return pltpu.make_async_copy(
            frames_ref.at[:, :, pl.ds(pl.multiple_of(visit * low_cols, low_cols), low_cols)],
            frame_ref.at[0],
            local_sem.at[1],
        )

    own_frames().start()

    up, down = (sky > 0).astype(jnp.int32), (sky < sky_count - 1).astype(jnp.int32)
    left, right = (visit > 0).astype(jnp.int32), (visit < visit_count - 1).astype(jnp.int32)
    pl.semaphore_wait(barrier, visit_count - 1 + (up + down) * (1 + left + right))

    def halo_copy(n, y, x):
        return pltpu.make_async_remote_copy(
            src_ref=model_ref.at[edge_of(y, x)],
            dst_ref=grid_ref.at[row_part(-y), col_part(-x)],
            send_sem=halo_send.at[n],
            recv_sem=halo_recv.at[n],
            device_id=device(y, x),
            device_id_type=pl.DeviceIdType.MESH,
        )

    def frame_copy(o):
        peer = peer_of(o)
        return pltpu.make_async_remote_copy(
            src_ref=frames_ref.at[:, :, pl.ds(pl.multiple_of(peer * low_cols, low_cols), low_cols)],
            dst_ref=frame_ref.at[o],
            send_sem=frame_send.at[o],
            recv_sem=frame_recv.at[o],
            device_id=(tile, sky, peer),
            device_id_type=pl.DeviceIdType.MESH,
        )

    for n, (y, x) in enumerate(NEIGHBOURS):

        @pl.when(exists(y, x))
        def _():
            halo_copy(n, y, x).start()

    def send_frames(o, carry):
        frame_copy(o).start()
        return carry

    lax.fori_loop(1, visit_count, send_frames, 0)

    for y, x in NEIGHBOURS:

        @pl.when(jnp.logical_not(exists(y, x)))
        def _():
            part = (row_part(y), col_part(x))
            grid_ref[part] = jnp.zeros(grid_ref.at[part].shape, jnp.float32)

    margin = (clipped_ref.shape[0] - low_rows) // 2
    clipped_ref[0:margin, :] = jnp.zeros((margin, low_cols), jnp.float32)
    clipped_ref[margin + low_rows :, :] = jnp.zeros((margin, low_cols), jnp.float32)
    total_ref[...] = jnp.zeros(total_ref.shape, jnp.float32)
    spread = selection(
        (2 * LANES, 2 * LANES),
        lambda a, b: a == jnp.where(b < LANES, 2 * b, 2 * b - (2 * LANES - 1)),
    )
    join = selection(
        (2 * LANES, 2 * LANES),
        lambda a, b: b == jnp.where(a < LANES, 2 * a, 2 * a - (2 * LANES - 1)),
    )

    def folded(b):
        return jnp.where(b >= full_rows, b - full_rows, b)

    part_rows = selection(
        (full_rows, 2 * full_rows),
        lambda a, b: folded(b) == jnp.where(a < half_rows, 2 * a, 2 * a - (full_rows - 1)),
    )
    join_rows = selection(
        (full_rows, 2 * full_rows),
        lambda a, b: a == jnp.where(folded(b) < half_rows, 2 * folded(b), 2 * folded(b) - (full_rows - 1)),
    )

    own_model.wait()
    for n, (y, x) in enumerate(NEIGHBOURS):
        @pl.when(exists(-y, -x))
        def _():
            halo_copy(n, y, x).wait_recv()

    for n in range(blocks):
        block = split_rows(grid_ref[:, 2 * LANES * n : 2 * LANES * (n + 1)])
        apart = dot(part_rows, dot(block, spread).astype(jnp.bfloat16))
        whole_ref[:, LANES * n : LANES * (n + 1)] = apart[:, :LANES]
        whole_ref[:, half_cols + LANES * n : half_cols + LANES * (n + 1)] = apart[:, LANES:]
    for d in range(SHIFTS):
        odd, step = (d - REACH) % 2, (d - REACH) // 2
        for p in range(2):
            value = whole_ref[half_rows * p : half_rows * (p + 1), half_cols * odd : half_cols * (odd + 1)]
            if step:
                value = pltpu.roll(value, (-step) % half_cols, 1)
            shifted_ref[d, p] = value[:, :low_cols]

    strip = 16

    def next_col(value):
        return pltpu.roll(value, full_cols - 1, 1)

    for t in range(height // strip):
        above = grid_ref[ROWS - 1 + strip * t : ROWS - 1 + strip * (t + 1), :]
        here = grid_ref[ROWS + strip * t : ROWS + strip * (t + 1), :]
        below = grid_ref[ROWS + 1 + strip * t : ROWS + 1 + strip * (t + 1), :]
        gx, gy = here - above, next_col(above) - above
        value = gx * lax.rsqrt(gx * gx + gy * gy + eps_flux)
        gx, gy = below - here, next_col(here) - here
        scale = lax.rsqrt(gx * gx + gy * gy + eps_flux)
        flux = gy * scale
        value = value - gx * scale + (pltpu.roll(flux, 1, 1) - flux)
        out_ref[strip * t : strip * (t + 1), :] = tv_weight * value[:, :width]

    own_frames().wait()
    low_index = sky * low_rows + lax.broadcasted_iota(jnp.int32, (low_rows, low_cols), 0)

    def taps(ref, k, offset):
        out = []
        for d in range(SHIFTS):
            at = d - REACH - offset + TAPS // 2
            value = ref[k, jnp.clip(at, 0, TAPS - 1)]
            out.append(jnp.where((at >= 0) & (at < TAPS), value, 0.0))
        return out

    def chunk(o, carry):
        @pl.when(o > 0)
        def _():
            frame_copy(o).wait_recv()

        owner = lax.rem(visit - o + visit_count, visit_count)
        col_taps = []
        for j in range(per_device):
            k = owner * per_device + j
            row_taps = taps(rows_ref, k, dither_ref[k, 0])
            col_shift = dither_ref[k, 1]
            col_taps.append(taps(cols_ref, k, col_shift))
            for p in range(2):
                value = None
                for b in range(TAPS):
                    piece = cols_ref[k, b] * shifted_ref[col_shift + (b - TAPS // 2 + REACH), p]
                    value = piece if value is None else value + piece
                blurred_ref[p] = value
            predicted = None
            for d in range(SHIFTS):
                odd, step = (d - REACH) % 2, (d - REACH) // 2
                begin = ROWS // 2 + step
                piece = row_taps[d] * blurred_ref[odd, begin : begin + low_rows, :]
                predicted = piece if predicted is None else predicted + piece
            cut = cut_ref[k]
            inside = (low_index >= footprint_ref[k, 0]) & (low_index < footprint_ref[k, 1])
            error = predicted - frame_ref[o, j].astype(jnp.float32)
            clipped_ref[margin : margin + low_rows, :] = jnp.where(
                inside, jnp.minimum(jnp.maximum(error, -cut), cut), 0.0
            )
            for p in range(2):
                value = None
                for d in range(SHIFTS):
                    odd, step = (d - REACH) % 2, (d - REACH) // 2
                    if odd == p:
                        begin = margin - ROWS // 2 - step
                        piece = row_taps[d] * clipped_ref[begin : begin + half_rows, :]
                        value = piece if value is None else value + piece
                back_ref[j, p] = value
        for p in range(2):
            for d in range(SHIFTS):
                value = total_ref[d, p, :, :low_cols]
                for j in range(per_device):
                    value = value + col_taps[j][d] * back_ref[j, p]
                total_ref[d, p, :, :low_cols] = value
        return carry

    lax.fori_loop(0, visit_count, chunk, 0)

    for odd in range(2):
        for p in range(2):
            value = None
            for d in range(SHIFTS):
                step = (d - REACH) // 2
                if (d - REACH) % 2 == odd:
                    piece = total_ref[d, p]
                    if step:
                        piece = pltpu.roll(piece, step % half_cols, 1)
                    value = piece if value is None else value + piece
            whole_ref[half_rows * p : half_rows * (p + 1), half_cols * odd : half_cols * (odd + 1)] = value
    for n in range(blocks):
        even = whole_ref[:, LANES * n : LANES * (n + 1)]
        odd = whole_ref[:, half_cols + LANES * n : half_cols + LANES * (n + 1)]
        block = split_rows(jnp.concatenate([even, odd], axis=1))
        grid_ref[:, 2 * LANES * n : 2 * LANES * (n + 1)] = dot(
            join_rows, dot(block, join).astype(jnp.bfloat16)
        )

    def landing(y, x):
        if x == 0:
            return end_ref.at[(y + 1) // 2]
        if y == 0:
            return side_ref.at[(x + 1) // 2]
        return corner_ref.at[(y + 1) + (x + 1) // 2]

    def fold_copy(n, y, x):
        return pltpu.make_async_remote_copy(
            src_ref=grid_ref.at[row_part(y), col_part(x)],
            dst_ref=landing(-y, -x),
            send_sem=fold_send.at[n],
            recv_sem=fold_recv.at[n],
            device_id=device(y, x),
            device_id_type=pl.DeviceIdType.MESH,
        )

    for n, (y, x) in enumerate(NEIGHBOURS):

        @pl.when(exists(y, x))
        def _():
            fold_copy(n, y, x).start()

    scale = 1.0 / float(visits) ** 0.5
    out_ref[...] += scale * grid_ref[ROWS : ROWS + height, 0:width]
    for n, (y, x) in enumerate(NEIGHBOURS):

        @pl.when(exists(-y, -x))
        def _():
            fold_copy(n, y, x).wait_recv()
            part = edge_of(-y, -x)
            out_ref[part] += scale * landing(-y, -x)[...]

    for n, (y, x) in enumerate(NEIGHBOURS):

        @pl.when(exists(y, x))
        def _():
            halo_copy(n, y, x).wait_send()
            fold_copy(n, y, x).wait_send()

    def sent(o, carry):
        frame_copy(o).wait_send()
        return carry

    lax.fori_loop(1, visit_count, sent, 0)


def solution(mesh):
    in_specs = (
        P(("tiles", "sky"), "visit"),
        P(("tiles", "visit"), "sky", None),
        P("tiles", None),
        P("tiles", None),
        P("tiles", None),
        P("tiles", None),
        P("tiles"),
    )
    out_specs = P(("tiles", "sky"), "visit")
    sky_count, visit_count = mesh.shape["sky"], mesh.shape["visit"]

    def on_device(sky_model, frames, psf_rows, psf_cols, dither, footprint, huber_cut):
        height, width = sky_model.shape
        per_device, low_rows = frames.shape[:2]
        low_cols = frames.shape[2] // visit_count
        half_rows, half_cols = height // 2 + ROWS, width // 2 + LANES
        f32 = jnp.float32
        return pl.pallas_call(
            functools.partial(kernel, (sky_count, visit_count)),
            out_shape=jax.ShapeDtypeStruct((height, width), f32),
            in_specs=[pl.BlockSpec(memory_space=pl.ANY)] * 2
            + [pl.BlockSpec(memory_space=pltpu.SMEM)] * 5,
            out_specs=pl.BlockSpec(memory_space=pltpu.VMEM),
            scratch_shapes=[
                pltpu.VMEM((height + 2 * ROWS, width + 2 * LANES), f32),
                pltpu.VMEM((SHIFTS, 2, half_rows, low_cols), f32),
                pltpu.VMEM((visit_count, per_device, low_rows, low_cols), jnp.bfloat16),
                pltpu.VMEM((2, half_rows, low_cols), f32),
                pltpu.VMEM((low_rows + 16, low_cols), f32),
                pltpu.VMEM((per_device, 2, half_rows, low_cols), f32),
                pltpu.VMEM((SHIFTS, 2, half_rows, half_cols), f32),
                pltpu.VMEM((height + 2 * ROWS, width + 2 * LANES), f32),
                pltpu.VMEM((2, height, LANES), f32),
                pltpu.VMEM((2, ROWS, width), f32),
                pltpu.VMEM((4, ROWS, LANES), f32),
                pltpu.SemaphoreType.DMA((2,)),
                pltpu.SemaphoreType.DMA((8,)),
                pltpu.SemaphoreType.DMA((8,)),
                pltpu.SemaphoreType.DMA((visit_count,)),
                pltpu.SemaphoreType.DMA((visit_count,)),
                pltpu.SemaphoreType.DMA((8,)),
                pltpu.SemaphoreType.DMA((8,)),
            ],
            compiler_params=pltpu.CompilerParams(
                collective_id=0, has_side_effects=True, vmem_limit_bytes=32 * 1024 * 1024
            ),
        )(sky_model, frames, psf_rows, psf_cols, dither, footprint, huber_cut)

    return jax.shard_map(
        on_device, mesh=mesh, in_specs=in_specs, out_specs=out_specs, check_vma=False
    )
```

time: 259 us -> 24.1 us (0.09)
  waiting for transfers between devices: 63.1 us -> 0 us
  local copies, waits for them, and re-layouts: 65.4 us -> 4.06 us
  other arithmetic: 54.1 us -> 0 us
  loops' own time: 48.8 us -> 0 us
  Pallas kernels: 0 us -> 19.8 us
  between operations: 13.5 us -> 0.02 us
  starting transfers between devices: 12.2 us -> 0 us
    another operation x1 -> x0, loops' own time: 48.8 us -> none  [on_device(): lax.fori_loop(0, per_device, one_visit, jnp.zeros((height + 2 * margin, f...]
    slice x11 -> x0, local copies, waits for them, and re-layouts: 37.2 us -> none  [the longest x2 22.1 us: blur_down(): return accum[::2]]
    add x7 -> x0, other arithmetic: 34.1 us -> none  [the longest x4 22.4 us: blur_down(): accum = piece if accum is None else accum + piece]
    all_gather x1 -> x0, waiting for transfers between devices: 29.8 us -> none  [on_device(): whole = lax.all_gather(with_rows, 'visit', axis=1, tiled=True)]
    reduce_scatter x1 -> x0, waiting for transfers between devices: 28.8 us -> none  [on_device(): lax.psum_scatter(partial_sum, 'visit', scatter_dimension=1, tiled=True)]
    pallas_call x0 -> x1, Pallas kernels: none -> 19.8 us  [on_device(): pl.pallas_call(functools.partial(kernel, (sky_count, visit_count)), out_s...]
    while x13 -> x0, local copies, waits for them, and re-layouts: 14.7 us -> none
    another operation x4 -> x0, other arithmetic: 14.3 us -> none  [the longest x2 8.62 us: spread_up(): jnp.stack([small, blank], 2).reshape(small.shape[0], 2 * small.shape[1])]
  transfers between devices with their start and end apart: 6 -> 0, of which waited for: 4 -> 0; matrix products, arithmetic and copies ran while one was open for 1% -> 0% of each run, Pallas kernels for 0% -> 0%
where the time goes in v1:
time: 24.1 us; the launch traced here: 23.9 us
  Pallas kernels  19.8 us (82%)
  local copies, waits for them, and re-layouts  4.06 us (17%)
    pallas_call x1, Pallas kernels, on_device(): pl.pallas_call(functools.partial(kernel, (sky_count, visit_count)), out_s...  19.8 us
    unnamed x15, local copies, waits for them, and re-layouts  4.06 us

profile of v1, /device:TPU:1, one launch (start us, length us, event | category | flops | bytes accessed | tf_op | source)
XLA Modules:
  0.0 23.9 jit_solution(11140581137647228509)
XLA Ops:
  0.0 0.0 copy-start.5
  0.0 0.0 copy-start.3
  0.0 0.0 copy-start.2
  0.0 0.8 %copy.8.dither_ref = s32[8,2]{1,0:T(8,128)S(1)} copy(s32[8,2]{0,1:T(2,128)} %param.11) | data formatting | bytes 128 | tf_op args[4]
  0.8 0.0 copy-done.5
  0.8 0.0 copy-start.4
  0.8 0.1 copy.9.footprint_ref
  0.9 0.0 copy-done.3
  0.9 0.0 copy-done.2
  0.9 0.6 %copy-done.4 = f32[8]{0:T(128)S(1)} copy-done((f32[8]{0:T(128)S(1)}, f32[8]{0:T(128)}, u32[]{:S(2)}) %copy-start.4) | copy-done | bytes 56
  1.5 0.0 copy-start
  1.5 0.9 %copy-done = f32[64,1024]{1,0:T(8,128)S(1)} copy-done((f32[64,1024]{1,0:T(8,128)S(1)}, f32[64,1024]{1,0:T(8,128)}, u32[]{:S(2)}) %copy-start) | copy-done | bytes 262168
  2.4 0.0 copy-start.1
  2.4 0.9 %copy-done.1 = bf16[2,32,2048]{2,1,0:T(8,128)(2,1)S(1)} copy-done((bf16[2,32,2048]{2,1,0:T(8,128)(2,1)S(1)}, bf16[2,32,2048]{2,1,0:T(8,128)(2,1)}, u32[]{:S(2)}) %copy-start.1) | copy-done | bytes 262168
  3.4 19.8 %shard_map.73 = f32[64,1024]{1,0:T(8,128)S(1)} custom-call(f32[64,1024]{1,0:T(8,128)S(1)} %copy-done, bf16[2,32,2048]{2,1,0:T(8,128)(2,1)S(1)} %copy-done.1, f32[8,5]{1,0:T(8,128)S(1)} %copy-done.2, f32[8,5]{1,0:T(8,128)S(1)} %copy-done.3, s32[8,2]{1,0:T(8,128)S(1)} %copy.8.dither_ref, s32[8,2]{1,0:T(8,128)S(1)} %copy.9.footprint_ref, f32[8]{0:T(128)S(1)} %copy-done.4), custom_call_target="tpu_custom_call" | custom-call | tf_op jit(solution)/shard_map/pallas_call | solution.py:386
  23.2 0.7 %copy.11 = f32[64,1024]{1,0:T(8,128)} copy(f32[64,1024]{1,0:T(8,128)S(1)} %shard_map.73) | data formatting | bytes 524288
Async XLA Ops:
  0.0 0.8 %copy-start.5 = (s32[8,2]{0,1:T(2,128)S(1)}, s32[8,2]{0,1:T(2,128)}, u32[]{:S(2)}) copy-start(s32[8,2]{0,1:T(2,128)} %param.12) | copy-start | bytes 196
  0.0 0.9 %copy-start.3 = (f32[8,5]{1,0:T(8,128)S(1)}, f32[8,5]{1,0:T(8,128)}, u32[]{:S(2)}) copy-start(f32[8,5]{1,0:T(8,128)} %cols_ref.1) | copy-start | bytes 484
  0.0 0.9 %copy-start.2 = (f32[8,5]{1,0:T(8,128)S(1)}, f32[8,5]{1,0:T(8,128)}, u32[]{:S(2)}) copy-start(f32[8,5]{1,0:T(8,128)} %rows_ref.1) | copy-start | bytes 484
  0.8 0.7 %copy-start.4 = (f32[8]{0:T(128)S(1)}, f32[8]{0:T(128)}, u32[]{:S(2)}) copy-start(f32[8]{0:T(128)} %cut_ref.1) | copy-start | bytes 100
  1.5 0.9 %copy-start = (f32[64,1024]{1,0:T(8,128)S(1)}, f32[64,1024]{1,0:T(8,128)}, u32[]{:S(2)}) copy-start(f32[64,1024]{1,0:T(8,128)} %model_ref.1) | copy-start | bytes 786436
  2.4 0.9 %copy-start.1 = (bf16[2,32,2048]{2,1,0:T(8,128)(2,1)S(1)}, bf16[2,32,2048]{2,1,0:T(8,128)(2,1)}, u32[]{:S(2)}) copy-start(bf16[2,32,2048]{2,1,0:T(8,128)(2,1)} %frames_ref.1) | copy-start | bytes 786436

commit v2 on v1

--- a/solution.py
+++ b/solution.py
@@ -40,12 +40,19 @@
     counts,
     model_ref,
     frames_ref,
+    rows_in,
+    cols_in,
+    dither_in,
+    footprint_in,
+    cut_in,
+    out_ref,
     rows_ref,
     cols_ref,
     dither_ref,
     footprint_ref,
     cut_ref,
-    out_ref,
+    row_taps,
+    col_taps,
     grid_ref,
     shifted_ref,
     frame_ref,
@@ -58,6 +65,7 @@
     end_ref,
     corner_ref,
     local_sem,
+    small_sem,
     halo_send,
     halo_recv,
     frame_send,
@@ -119,6 +127,20 @@
                     barrier, inc=1, device_id=device(y, x), device_id_type=pl.DeviceIdType.MESH
                 )
 
+    small = [
+        pltpu.make_async_copy(source, target, small_sem.at[n])
+        for n, (source, target) in enumerate(
+            (
+                (rows_in, rows_ref),
+                (cols_in, cols_ref),
+                (dither_in, dither_ref),
+                (footprint_in, footprint_ref),
+                (cut_in, cut_ref),
+            )
+        )
+    ]
+    for copy in small:
+        copy.start()
     own_model = pltpu.make_async_copy(
         model_ref, grid_ref.at[pl.ds(ROWS, height), pl.ds(0, width)], local_sem.at[0]
     )
@@ -132,6 +154,19 @@
         )
 
     own_frames().start()
+
+    for copy in small:
+        copy.wait()
+
+    def place(k, carry):
+        for ref, offset, placed in ((rows_ref, dither_ref[0, k], row_taps), (cols_ref, dither_ref[1, k], col_taps)):
+            for d in range(SHIFTS):
+                at = d - REACH - offset + TAPS // 2
+                value = ref[k, jnp.clip(at, 0, TAPS - 1)]
+                placed[k, d] = jnp.where((at >= 0) & (at < TAPS), value, 0.0)
+        return carry
+
+    lax.fori_loop(0, visits, place, 0)
 
     up, down = (sky > 0).astype(jnp.int32), (sky < sky_count - 1).astype(jnp.int32)
     left, right = (visit > 0).astype(jnp.int32), (visit < visit_count - 1).astype(jnp.int32)
@@ -241,26 +276,15 @@
     own_frames().wait()
     low_index = sky * low_rows + lax.broadcasted_iota(jnp.int32, (low_rows, low_cols), 0)
 
-    def taps(ref, k, offset):
-        out = []
-        for d in range(SHIFTS):
-            at = d - REACH - offset + TAPS // 2
-            value = ref[k, jnp.clip(at, 0, TAPS - 1)]
-            out.append(jnp.where((at >= 0) & (at < TAPS), value, 0.0))
-        return out
-
     def chunk(o, carry):
         @pl.when(o > 0)
         def _():
             frame_copy(o).wait_recv()
 
         owner = lax.rem(visit - o + visit_count, visit_count)
-        col_taps = []
         for j in range(per_device):
             k = owner * per_device + j
-            row_taps = taps(rows_ref, k, dither_ref[k, 0])
-            col_shift = dither_ref[k, 1]
-            col_taps.append(taps(cols_ref, k, col_shift))
+            col_shift = dither_ref[1, k]
             for p in range(2):
                 value = None
                 for b in range(TAPS):
@@ -271,10 +295,10 @@
             for d in range(SHIFTS):
                 odd, step = (d - REACH) % 2, (d - REACH) // 2
                 begin = ROWS // 2 + step
-                piece = row_taps[d] * blurred_ref[odd, begin : begin + low_rows, :]
+                piece = row_taps[k, d] * blurred_ref[odd, begin : begin + low_rows, :]
                 predicted = piece if predicted is None else predicted + piece
             cut = cut_ref[k]
-            inside = (low_index >= footprint_ref[k, 0]) & (low_index < footprint_ref[k, 1])
+            inside = (low_index >= footprint_ref[0, k]) & (low_index < footprint_ref[1, k])
             error = predicted - frame_ref[o, j].astype(jnp.float32)
             clipped_ref[margin : margin + low_rows, :] = jnp.where(
                 inside, jnp.minimum(jnp.maximum(error, -cut), cut), 0.0
@@ -285,15 +309,21 @@
                     odd, step = (d - REACH) % 2, (d - REACH) // 2
                     if odd == p:
                         begin = margin - ROWS // 2 - step
-                        piece = row_taps[d] * clipped_ref[begin : begin + half_rows, :]
+                        piece = row_taps[k, d] * clipped_ref[begin : begin + half_rows, :]
                         value = piece if value is None else value + piece
                 back_ref[j, p] = value
+        weights = [
+            [col_taps[owner * per_device + j, d] for d in range(SHIFTS)] for j in range(per_device)
+        ]
         for p in range(2):
-            for d in range(SHIFTS):
-                value = total_ref[d, p, :, :low_cols]
-                for j in range(per_device):
-                    value = value + col_taps[j][d] * back_ref[j, p]
-                total_ref[d, p, :, :low_cols] = value
+            for t in range(half_rows // 8):
+                rows = slice(8 * t, 8 * (t + 1))
+                back = [back_ref[j, p, rows] for j in range(per_device)]
+                for d in range(SHIFTS):
+                    value = total_ref[d, p, rows, :low_cols]
+                    for j in range(per_device):
+                        value = value + weights[j][d] * back[j]
+                    total_ref[d, p, rows, :low_cols] = value
         return carry
 
     lax.fori_loop(0, visit_count, chunk, 0)
@@ -309,14 +339,6 @@
                         piece = pltpu.roll(piece, step % half_cols, 1)
                     value = piece if value is None else value + piece
             whole_ref[half_rows * p : half_rows * (p + 1), half_cols * odd : half_cols * (odd + 1)] = value
-    for n in range(blocks):
-        even = whole_ref[:, LANES * n : LANES * (n + 1)]
-        odd = whole_ref[:, half_cols + LANES * n : half_cols + LANES * (n + 1)]
-        block = split_rows(jnp.concatenate([even, odd], axis=1))
-        grid_ref[:, 2 * LANES * n : 2 * LANES * (n + 1)] = dot(
-            join_rows, dot(block, join).astype(jnp.bfloat16)
-        )
-
     def landing(y, x):
         if x == 0:
             return end_ref.at[(y + 1) // 2]
@@ -334,11 +356,24 @@
             device_id_type=pl.DeviceIdType.MESH,
         )
 
-    for n, (y, x) in enumerate(NEIGHBOURS):
-
-        @pl.when(exists(y, x))
-        def _():
-            fold_copy(n, y, x).start()
+    def fold_start(beside):
+        for n, (y, x) in enumerate(NEIGHBOURS):
+            if (x != 0) == beside:
+
+                @pl.when(exists(y, x))
+                def _():
+                    fold_copy(n, y, x).start()
+
+    for n in reversed(range(blocks)):
+        even = whole_ref[:, LANES * n : LANES * (n + 1)]
+        odd = whole_ref[:, half_cols + LANES * n : half_cols + LANES * (n + 1)]
+        block = split_rows(jnp.concatenate([even, odd], axis=1))
+        grid_ref[:, 2 * LANES * n : 2 * LANES * (n + 1)] = dot(
+            join_rows, dot(block, join).astype(jnp.bfloat16)
+        )
+        if n == blocks - 1:
+            fold_start(True)
+    fold_start(False)
 
     scale = 1.0 / float(visits) ** 0.5
     out_ref[...] += scale * grid_ref[ROWS : ROWS + height, 0:width]
@@ -380,16 +415,23 @@
     def on_device(sky_model, frames, psf_rows, psf_cols, dither, footprint, huber_cut):
         height, width = sky_model.shape
         per_device, low_rows = frames.shape[:2]
+        visits = psf_rows.shape[0]
         low_cols = frames.shape[2] // visit_count
         half_rows, half_cols = height // 2 + ROWS, width // 2 + LANES
         f32 = jnp.float32
         return pl.pallas_call(
             functools.partial(kernel, (sky_count, visit_count)),
             out_shape=jax.ShapeDtypeStruct((height, width), f32),
-            in_specs=[pl.BlockSpec(memory_space=pl.ANY)] * 2
-            + [pl.BlockSpec(memory_space=pltpu.SMEM)] * 5,
+            in_specs=[pl.BlockSpec(memory_space=pltpu.HBM)] * 7,
             out_specs=pl.BlockSpec(memory_space=pltpu.VMEM),
             scratch_shapes=[
+                pltpu.SMEM(psf_rows.shape, f32),
+                pltpu.SMEM(psf_cols.shape, f32),
+                pltpu.SMEM(dither.shape[::-1], jnp.int32),
+                pltpu.SMEM(footprint.shape[::-1], jnp.int32),
+                pltpu.SMEM(huber_cut.shape, f32),
+                pltpu.SMEM((visits, SHIFTS), f32),
+                pltpu.SMEM((visits, SHIFTS), f32),
                 pltpu.VMEM((height + 2 * ROWS, width + 2 * LANES), f32),
                 pltpu.VMEM((SHIFTS, 2, half_rows, low_cols), f32),
                 pltpu.VMEM((visit_count, per_device, low_rows, low_cols), jnp.bfloat16),
@@ -402,6 +444,7 @@
                 pltpu.VMEM((2, ROWS, width), f32),
                 pltpu.VMEM((4, ROWS, LANES), f32),
                 pltpu.SemaphoreType.DMA((2,)),
+                pltpu.SemaphoreType.DMA((5,)),
                 pltpu.SemaphoreType.DMA((8,)),
                 pltpu.SemaphoreType.DMA((8,)),
                 pltpu.SemaphoreType.DMA((visit_count,)),
@@ -410,9 +453,9 @@
                 pltpu.SemaphoreType.DMA((8,)),
             ],
             compiler_params=pltpu.CompilerParams(
-                collective_id=0, has_side_effects=True, vmem_limit_bytes=32 * 1024 * 1024
+                collective_id=0, has_side_effects=True, vmem_limit_bytes=63 * 1024 * 1024
             ),
-        )(sky_model, frames, psf_rows, psf_cols, dither, footprint, huber_cut)
+        )(sky_model, frames, psf_rows, psf_cols, dither.T, footprint.T, huber_cut)
 
     return jax.shard_map(
         on_device, mesh=mesh, in_specs=in_specs, out_specs=out_specs, check_vma=False

time: 24.1 us -> 21.1 us (0.88)
  local copies, waits for them, and re-layouts: 4.06 us -> 1.67 us
  Pallas kernels: 19.8 us -> 19.2 us
    unnamed x15 -> x1, local copies, waits for them, and re-layouts: 4.06 us -> 1.67 us
    pallas_call x1, Pallas kernels: 19.8 us -> 19.2 us  [on_device(): pl.pallas_call(functools.partial(kernel, (sky_count, visit_count)), out_s...]
where the time goes in v2:
time: 21.1 us; the launch traced here: 20.9 us
  Pallas kernels  19.2 us (91%)
  local copies, waits for them, and re-layouts  1.67 us (8%)
    pallas_call x1, Pallas kernels, on_device(): pl.pallas_call(functools.partial(kernel, (sky_count, visit_count)), out_s...  19.2 us
    unnamed x1, local copies, waits for them, and re-layouts  1.67 us

profile of v2, /device:TPU:1, one launch (start us, length us, event | category | flops | bytes accessed | tf_op | source)
XLA Modules:
  0.0 20.9 jit_solution(1804190800454197810)
XLA Ops:
  0.0 19.2 %shard_map.73 = f32[64,1024]{1,0:T(8,128)} custom-call(f32[64,1024]{1,0:T(8,128)} %model_ref.1, bf16[2,32,2048]{2,1,0:T(8,128)(2,1)} %frames_ref.1, f32[8,5]{1,0:T(8,128)} %rows_in.1, f32[8,5]{1,0:T(8,128)} %cols_in.1, s32[2,8]{1,0:T(2,128)} %bitcast.2, s32[2,8]{1,0:T(2,128)} %bitcast.3, f32[8]{0:T(128)} %cut_in.1), custom_call_target="tpu_custom_call" | custom-call | tf_op jit(solution)/shard_map/pallas_call | solution.py:422
  19.2 1.7 %copy.9 = f32[64,1024]{1,0:T(8,128)} copy(f32[64,1024]{1,0:T(8,128)} %shard_map.73) | data formatting | bytes 524288

commit v3 on v2

--- a/solution.py
+++ b/solution.py
@@ -61,6 +61,9 @@
     back_ref,
     total_ref,
     whole_ref,
+    sum_ref,
+    side_out,
+    side_in,
     side_ref,
     end_ref,
     corner_ref,
@@ -168,11 +171,33 @@
 
     lax.fori_loop(0, visits, place, 0)
 
+    lane = lax.broadcasted_iota(jnp.int32, (8, LANES), 1)
+    own_model.wait()
+    for side in range(2):
+        packed = jnp.zeros((8, LANES), jnp.float32)
+        begin = (width - LANES) * side
+        for t in range(height // 8):
+            piece = grid_ref[ROWS + 8 * t : ROWS + 8 * (t + 1), begin : begin + LANES]
+            shift = (8 * t + 8 * side) % LANES
+            piece = pltpu.roll(piece, shift, 1) if shift else piece
+            packed = jnp.where((lane >= 8 * t) & (lane < 8 * t + 8), piece, packed)
+        side_out[side] = packed
+
     up, down = (sky > 0).astype(jnp.int32), (sky < sky_count - 1).astype(jnp.int32)
     left, right = (visit > 0).astype(jnp.int32), (visit < visit_count - 1).astype(jnp.int32)
     pl.semaphore_wait(barrier, visit_count - 1 + (up + down) * (1 + left + right))
 
     def halo_copy(n, y, x):
+        if y == 0:
+            side = (x + 1) // 2
+            return pltpu.make_async_remote_copy(
+                src_ref=side_out.at[side],
+                dst_ref=side_in.at[side],
+                send_sem=halo_send.at[n],
+                recv_sem=halo_recv.at[n],
+                device_id=device(y, x),
+                device_id_type=pl.DeviceIdType.MESH,
+            )
         return pltpu.make_async_remote_copy(
             src_ref=model_ref.at[edge_of(y, x)],
             dst_ref=grid_ref.at[row_part(-y), col_part(-x)],
@@ -237,11 +262,21 @@
         lambda a, b: a == jnp.where(folded(b) < half_rows, 2 * folded(b), 2 * folded(b) - (full_rows - 1)),
     )
 
-    own_model.wait()
     for n, (y, x) in enumerate(NEIGHBOURS):
         @pl.when(exists(-y, -x))
         def _():
             halo_copy(n, y, x).wait_recv()
+            if y == 0:
+                side = (x + 1) // 2
+                packed = side_in[side]
+                begin = width + LANES * side
+                for t in range(height // 8):
+                    shift = (-8 * t - 8 * side) % LANES
+                    piece = pltpu.roll(packed, shift, 1) if shift else packed
+                    keep = lane >= LANES - 8 if side else lane < 8
+                    grid_ref[ROWS + 8 * t : ROWS + 8 * (t + 1), begin : begin + LANES] = jnp.where(
+                        keep, piece, 0.0
+                    )
 
     for n in range(blocks):
         block = split_rows(grid_ref[:, 2 * LANES * n : 2 * LANES * (n + 1)])
@@ -255,23 +290,6 @@
             if step:
                 value = pltpu.roll(value, (-step) % half_cols, 1)
             shifted_ref[d, p] = value[:, :low_cols]
-
-    strip = 16
-
-    def next_col(value):
-        return pltpu.roll(value, full_cols - 1, 1)
-
-    for t in range(height // strip):
-        above = grid_ref[ROWS - 1 + strip * t : ROWS - 1 + strip * (t + 1), :]
-        here = grid_ref[ROWS + strip * t : ROWS + strip * (t + 1), :]
-        below = grid_ref[ROWS + 1 + strip * t : ROWS + 1 + strip * (t + 1), :]
-        gx, gy = here - above, next_col(above) - above
-        value = gx * lax.rsqrt(gx * gx + gy * gy + eps_flux)
-        gx, gy = below - here, next_col(here) - here
-        scale = lax.rsqrt(gx * gx + gy * gy + eps_flux)
-        flux = gy * scale
-        value = value - gx * scale + (pltpu.roll(flux, 1, 1) - flux)
-        out_ref[strip * t : strip * (t + 1), :] = tv_weight * value[:, :width]
 
     own_frames().wait()
     low_index = sky * low_rows + lax.broadcasted_iota(jnp.int32, (low_rows, low_cols), 0)
@@ -348,7 +366,7 @@
 
     def fold_copy(n, y, x):
         return pltpu.make_async_remote_copy(
-            src_ref=grid_ref.at[row_part(y), col_part(x)],
+            src_ref=sum_ref.at[row_part(y), col_part(x)],
             dst_ref=landing(-y, -x),
             send_sem=fold_send.at[n],
             recv_sem=fold_recv.at[n],
@@ -368,22 +386,40 @@
         even = whole_ref[:, LANES * n : LANES * (n + 1)]
         odd = whole_ref[:, half_cols + LANES * n : half_cols + LANES * (n + 1)]
         block = split_rows(jnp.concatenate([even, odd], axis=1))
-        grid_ref[:, 2 * LANES * n : 2 * LANES * (n + 1)] = dot(
+        sum_ref[:, 2 * LANES * n : 2 * LANES * (n + 1)] = dot(
             join_rows, dot(block, join).astype(jnp.bfloat16)
         )
         if n == blocks - 1:
             fold_start(True)
     fold_start(False)
 
-    scale = 1.0 / float(visits) ** 0.5
-    out_ref[...] += scale * grid_ref[ROWS : ROWS + height, 0:width]
+    share = 1.0 / float(visits) ** 0.5
+
+    strip = 16
+
+    def next_col(value):
+        return pltpu.roll(value, full_cols - 1, 1)
+
+    for t in range(height // strip):
+        above = grid_ref[ROWS - 1 + strip * t : ROWS - 1 + strip * (t + 1), :]
+        here = grid_ref[ROWS + strip * t : ROWS + strip * (t + 1), :]
+        below = grid_ref[ROWS + 1 + strip * t : ROWS + 1 + strip * (t + 1), :]
+        gx, gy = here - above, next_col(above) - above
+        value = gx * lax.rsqrt(gx * gx + gy * gy + eps_flux)
+        gx, gy = below - here, next_col(here) - here
+        scale = lax.rsqrt(gx * gx + gy * gy + eps_flux)
+        flux = gy * scale
+        value = value - gx * scale + (pltpu.roll(flux, 1, 1) - flux)
+        data = sum_ref[ROWS + strip * t : ROWS + strip * (t + 1), 0:width]
+        out_ref[strip * t : strip * (t + 1), :] = share * data + tv_weight * value[:, :width]
+
     for n, (y, x) in enumerate(NEIGHBOURS):
 
         @pl.when(exists(-y, -x))
         def _():
             fold_copy(n, y, x).wait_recv()
             part = edge_of(-y, -x)
-            out_ref[part] += scale * landing(-y, -x)[...]
+            out_ref[part] += share * landing(-y, -x)[...]
 
     for n, (y, x) in enumerate(NEIGHBOURS):
 
@@ -440,6 +476,9 @@
                 pltpu.VMEM((per_device, 2, half_rows, low_cols), f32),
                 pltpu.VMEM((SHIFTS, 2, half_rows, half_cols), f32),
                 pltpu.VMEM((height + 2 * ROWS, width + 2 * LANES), f32),
+                pltpu.VMEM((height + 2 * ROWS, width + 2 * LANES), f32),
+                pltpu.VMEM((2, 8, LANES), f32),
+                pltpu.VMEM((2, 8, LANES), f32),
                 pltpu.VMEM((2, height, LANES), f32),
                 pltpu.VMEM((2, ROWS, width), f32),
                 pltpu.VMEM((4, ROWS, LANES), f32),

time: 21.1 us -> 20.5 us (0.972)
  Pallas kernels: 19.2 us -> 18.6 us
    pallas_call x1, Pallas kernels: 19.2 us -> 18.6 us  [on_device(): pl.pallas_call(functools.partial(kernel, (sky_count, visit_count)), out_s...]
where the time goes in v3:
time: 20.5 us; the launch traced here: 20.3 us
  Pallas kernels  18.6 us (91%)
  local copies, waits for them, and re-layouts  1.67 us (8%)
    pallas_call x1, Pallas kernels, on_device(): pl.pallas_call(functools.partial(kernel, (sky_count, visit_count)), out_s...  18.6 us
    unnamed x1, local copies, waits for them, and re-layouts  1.67 us

profile of v3, /device:TPU:1, one launch (start us, length us, event | category | flops | bytes accessed | tf_op | source)
XLA Modules:
  0.0 20.3 jit_solution(13716735745495262394)
XLA Ops:
  0.0 18.6 %shard_map.73 = f32[64,1024]{1,0:T(8,128)} custom-call(f32[64,1024]{1,0:T(8,128)} %model_ref.1, bf16[2,32,2048]{2,1,0:T(8,128)(2,1)} %frames_ref.1, f32[8,5]{1,0:T(8,128)} %rows_in.1, f32[8,5]{1,0:T(8,128)} %cols_in.1, s32[2,8]{1,0:T(2,128)} %bitcast.2, s32[2,8]{1,0:T(2,128)} %bitcast.3, f32[8]{0:T(128)} %cut_in.1), custom_call_target="tpu_custom_call" | custom-call | tf_op jit(solution)/shard_map/pallas_call | solution.py:458
  18.6 1.7 %copy.9 = f32[64,1024]{1,0:T(8,128)} copy(f32[64,1024]{1,0:T(8,128)} %shard_map.73) | data formatting | bytes 524288
